TPU v7x, 512 devices: a whole 4x4x16 slice. The times are simulated.
512 devices in a mesh: dp: 16 (over y, x), expert: 32 (over z, core).
Axes of the slice: x: 4, y: 4, z: 16, core: 2. Of those that a mesh axis runs over, the one named last changes fastest.
Arguments:
- panorama: bfloat16 [31, 768, 1664], P(None, 'expert', 'dp'), may hold values from -6 to 6
- tile_anchor: int32 [64, 2], P('expert'), may hold values from 0 to 7
- tile_count: int32 [32], P('expert'), may hold values from 1 to 2, as said below
- pre_attention_gain: float32 [1664], P('dp'), may hold values from 0.1 to 1.9
- qkv_weight: bfloat16 [3, 1664, 1664], P(None, None, 'dp'), may hold values from -0.21875 to 0.21875
- out_weight: bfloat16 [1664, 1664], P(None, 'dp'), may hold values from -0.21875 to 0.21875
- pre_expert_gain: float32 [1664], P('dp'), may hold values from 0.1 to 1.9
- router_weight: float32 [1664, 32], P('dp'), may hold values from -0.3125 to 0.3125
- expand_weight: bfloat16 [32, 1664, 8192], P('expert', None, 'dp'), may hold values from -0.15625 to 0.15625
- reduce_weight: bfloat16 [32, 8192, 1664], P('expert', 'dp'), may hold values from -0.09375 to 0.09375
- route_index: int32 [36864, 2], P('expert'), may hold values from 0 to 31, as said below
- slot_index: int32 [36864, 2], P('expert'), may hold values from -1 to 35, as said below
Outputs:
- panorama_out: bfloat16 [31, 768, 1664], P(None, 'expert', 'dp')
Inputs may be any that keep to these rules, and one draw needn't show every extreme that they name: `tile_count`: some tile column has 2 live tiles. `route_index`: each token names two different experts. `slot_index`: within one tile column, the kept assignments to one expert have distinct slots; every assignment of a token of a tile slot that is not live is dropped; in every draw one expert holds 36 kept assignments from every tile column.
All inputs are finite; a program needn't handle non-finite values.
Results may differ from a plain program's by a relative error of at most 0.0089.
Values may be sent and summed in bfloat16 or wider, within the bound.
A program may use at most 64 MiB of HBM per device.

v0:
```python
import jax
import jax.numpy as jnp
from jax import lax
from jax.sharding import Mesh
from jax.sharding import PartitionSpec as P

HEAD_DIM = 104
TILE_SIDE = 24
DP = ("dp_0", "dp_1")


def passed_along(block, axis, distance):
    devices = range(lax.axis_size(axis))
    route = [((i - distance) % len(devices), i) for i in devices]
    return lax.ppermute(block, axis, route)


def by_axis(x, axes):
    for axis in axes:
        x = lax.psum(x, axis)
    return x


def from_everyone(x, axis):
    length = lax.axis_size(axis)
    return lax.all_to_all(jnp.broadcast_to(x[None], (length, *x.shape)), axis, 0, 0, tiled=True)


def over_copies(x, axis):
    everything = from_everyone(x, axis)
    return jnp.sum(everything, axis=0)


def in_one(arrays, axis):
    ends = [0]
    for a in arrays:
        ends.append(ends[-1] + a.size)
    running = over_copies(jnp.concatenate([a.ravel() for a in arrays]), axis)
    return tuple((running[b:e].reshape(a.shape) for a, b, e in zip(arrays, ends, ends[1:])))


def in_blocks(x, dim, length):
    shape = x.shape
    pieces = x.reshape(*shape[:dim], length, shape[dim] // length, *shape[dim + 1 :])
    return jnp.moveaxis(pieces, dim, 0)


def sum_at_owner(x, axis, dim):
    length = lax.axis_size(axis)
    pieces = lax.all_to_all(in_blocks(x, dim, length), axis, 0, 0, tiled=True)
    return jnp.sum(pieces.astype(jnp.float32), axis=0)


def body(
    panorama,
    tile_anchor,
    tile_count,
    pre_attention_gain,
    qkv_weight,
    out_weight,
    pre_expert_gain,
    router_weight,
    expand_weight,
    reduce_weight,
    route_index,
    slot_index,
):
    dp_count = lax.axis_size(DP)
    expert_count = lax.axis_size("expert")
    height, own_width, features = panorama.shape
    full_width = features * dp_count
    tiles_here = tile_anchor.shape[0]
    tile_tokens = TILE_SIDE * TILE_SIDE
    column_tokens = tiles_here * tile_tokens
    experts = router_weight.shape[1]
    capacity = column_tokens // experts
    neighbour = passed_along(panorama, "expert", -1)
    area = jnp.concatenate([panorama, neighbour], axis=1).reshape(height * 2 * own_width, features)
    step_ids = jnp.arange(tile_tokens, dtype=jnp.int32)
    patch_rows = tile_anchor[:, 0:1] + (step_ids // TILE_SIDE)[None, :]
    patch_cols = tile_anchor[:, 1:2] + (step_ids % TILE_SIDE)[None, :]
    flat_index = (patch_rows * (2 * own_width) + patch_cols).reshape(column_tokens)
    live_tile = jnp.arange(tiles_here, dtype=jnp.int32) < tile_count[0]
    live_token = jnp.repeat(live_tile, tile_tokens)
    tokens = area[flat_index]
    tokens32 = tokens.astype(jnp.float32)
    first_sum, square_sum = (
        by_axis(jnp.sum(tokens32, axis=1), DP),
        by_axis(jnp.sum(tokens32 * tokens32, axis=1), DP),
    )
    mean_value = first_sum / full_width
    inverse_std = lax.rsqrt(square_sum / full_width - mean_value * mean_value + 1e-06)
    normed = ((tokens32 - mean_value[:, None]) * inverse_std[:, None] * pre_attention_gain).astype(
        jnp.bfloat16
    )
    weight_rows = qkv_weight
    projected = jnp.einsum(
        "tf,sfo->sto",
        lax.all_gather(normed, DP, axis=1, tiled=True),
        weight_rows,
        preferred_element_type=jnp.float32,
    ).astype(jnp.bfloat16)
    heads_here = features // HEAD_DIM
    shaped = projected.reshape(3, tiles_here, tile_tokens, heads_here, HEAD_DIM)
    scores = jnp.einsum(
        "aqhd,akhd->ahqk", shaped[0], shaped[1], preferred_element_type=jnp.float32
    ) * HEAD_DIM ** (-0.5)
    weights = jnp.exp(scores)
    weights = (weights / jnp.sum(weights, axis=-1, keepdims=True)).astype(jnp.bfloat16)
    attended = jnp.einsum("ahqk,akhd->aqhd", weights, shaped[2], preferred_element_type=jnp.float32)
    attended = attended.astype(jnp.bfloat16).reshape(column_tokens, features)
    weight_rows = out_weight
    mixed = tokens32 + jnp.dot(
        lax.all_gather(attended, DP, axis=1, tiled=True),
        weight_rows,
        preferred_element_type=jnp.float32,
    )
    chosen_mask = route_index[:, :, None] == jnp.arange(experts, dtype=jnp.int32)[None, None, :]

    def picked(table):
        return jnp.sum(jnp.where(chosen_mask, table[:, None, :], 0.0), axis=-1)

    direct = jnp.dot(mixed * pre_expert_gain, router_weight)
    gain_scores = jnp.dot(pre_expert_gain[None, :], router_weight)[0]
    first_sum, square_sum, direct_sum, gain_sum = in_one(
        (jnp.sum(mixed, axis=1), jnp.sum(mixed * mixed, axis=1), picked(direct), gain_scores), DP
    )
    mean_value = first_sum / full_width
    inverse_std = lax.rsqrt(square_sum / full_width - mean_value * mean_value + 1e-06)
    expert_in32 = (mixed - mean_value[:, None]) * inverse_std[:, None] * pre_expert_gain
    logits = inverse_std[:, None] * (direct_sum - mean_value[:, None] * picked(gain_sum[None, :]))
    gates = jax.nn.sigmoid(logits - logits[:, ::-1])
    expert_in = expert_in32.astype(jnp.bfloat16)
    keep = slot_index >= 0
    total_slots = experts * capacity
    target = jnp.where(keep, route_index * capacity + slot_index, total_slots)
    first_layer = expand_weight[0]
    second_layer = reduce_weight[0]
    sources = jnp.broadcast_to(expert_in[:, None, :], (column_tokens, 2, features))
    outbound = (
        jnp.zeros((total_slots + 1, features), jnp.bfloat16)
        .at[target.reshape(-1)]
        .set(sources.reshape(column_tokens * 2, features))[:total_slots]
        .reshape(experts, capacity, features)
    )
    inbound = lax.all_to_all(outbound, "expert", split_axis=0, concat_axis=0, tiled=True)
    slot_rows = inbound.reshape(expert_count * capacity, features)
    weight_rows = first_layer
    hidden_pre = jnp.dot(
        lax.all_gather(slot_rows, DP, axis=1, tiled=True),
        weight_rows,
        preferred_element_type=jnp.float32,
    )
    activated = jax.nn.gelu(hidden_pre, approximate=False).astype(jnp.bfloat16)
    expert_sum = sum_at_owner(
        jnp.einsum("hf,sh->fs", second_layer, activated, preferred_element_type=jnp.float32).astype(
            jnp.bfloat16
        ),
        DP,
        0,
    )
    returned = expert_sum.astype(jnp.bfloat16).reshape(features, expert_count, capacity)
    gathered_back = lax.all_to_all(
        returned, "expert", split_axis=1, concat_axis=1, tiled=True
    ).reshape(features, total_slots)
    fetched = jnp.take(gathered_back, jnp.where(keep, target, 0).reshape(-1), axis=1)
    fetched = fetched.reshape(features, column_tokens, 2).astype(jnp.float32)
    gate_weight = jnp.where(keep, gates, 0.0)
    expert_part = jnp.sum(fetched * gate_weight[None, :, :], axis=-1)
    final = mixed + expert_part.T
    out_index = jnp.where(live_token, flat_index, height * 2 * own_width)
    accumulated = (
        jnp.zeros((height * 2 * own_width + 1, features), jnp.float32).at[out_index].add(final)
    )
    accumulated = accumulated[: height * 2 * own_width].reshape(height, 2 * own_width, features)
    incoming = passed_along(accumulated[:, own_width:].astype(jnp.bfloat16), "expert", 1).astype(
        jnp.float32
    )
    return (accumulated[:, :own_width] + incoming).astype(jnp.bfloat16)


def solution(mesh):
    split = Mesh(mesh.devices.reshape(4, 4, mesh.shape["expert"]), ("dp_0", "dp_1", "expert"))
    return jax.shard_map(
        body,
        mesh=split,
        in_specs=(
            P(None, "expert", DP),
            P("expert", None),
            P("expert"),
            P(DP),
            P(None, None, DP),
            P(None, DP),
            P(DP),
            P(DP, None),
            P("expert", None, DP),
            P("expert", DP, None),
            P("expert", None),
            P("expert", None),
        ),
        out_specs=P(None, "expert", DP),
        check_vma=False,
    )
```

profile of v0, /device:TPU:24, one launch (start us, length us, event | category | flops | bytes accessed | tf_op | source)
XLA Modules:
  0.0 471.3 jit_solution(17326785341885395183)
XLA Ops:
  6.5 8.9 %collective-permute-start = (bf16[31,24,104]{2,1,0:T(8,128)(2,1)}, bf16[31,24,104]{2,1,0:T(8,128)(2,1)S(1)}, u32[]{:S(2)}, u32[]{:S(2)}) collective-permute-start(bf16[31,24,104]{2,1,0:T(8,128)(2,1)} %param.12), channel_id=1, source_target_pairs={{1,0},{2,1},{3,2},{4,3},{5,4},{6,5},{7,6},{8,7},{9,8},{10,9},{11,1... | collective-permute-start | bytes 464264 | tf_op jit(solution)/shard_map/ppermute | solution.py:15
  19.9 2.9 gather_fusion
  23.1 13.9 %all-reduce.1 = (f32[1152]{0:T(1024)S(1)}, f32[1152]{0:T(1024)S(1)}) all-reduce(f32[1152]{0:T(1024)S(1)} %get-tuple-element.8, f32[1152]{0:T(1024)S(1)} %get-tuple-element.7), channel_id=1, replica_groups=mesh['dp_0'=4,'dp_1'=4,'expert'=32] {'dp_0'}, use_global_device_ids=true, to_apply=%region_4.5 | all-reduce | flops 2304 | bytes 18432 | tf_op jit(solution)/shard_map/psum | solution.py:20
  37.0 16.9 %all-reduce = (f32[1152]{0:T(1024)S(1)}, f32[1152]{0:T(1024)S(1)}) all-reduce(f32[1152]{0:T(1024)S(1)} %get-tuple-element.15, f32[1152]{0:T(1024)S(1)} %get-tuple-element.16), channel_id=1, replica_groups=mesh['dp_0'=4,'dp_1'=4,'expert'=32] {'dp_1'}, use_global_device_ids=true, to_apply=%region_5.6 | all-reduce | flops 2304 | bytes 18432 | tf_op jit(solution)/shard_map/psum | solution.py:20
  54.8 59.1 %all-gather.4.cloned.1.call-done = bf16[1152,1664]{0,1:T(8,128)(2,1)} async-done(((bf16[1152,104]{0,1:T(8,128)(2,1)}), bf16[1152,1664]{0,1:T(8,128)(2,1)}) %all-gather.4.cloned.1.call-update) | async-done | bytes 3833872 | tf_op jit(solution)/shard_map/all_gather | solution.py:99
  113.9 4.0 fusion.119
  121.6 64.8 %all-gather.6.cloned.1.call-done = bf16[1152,1664]{0,1:T(8,128)(2,1)} async-done(((bf16[1152,104]{0,1:T(8,128)(2,1)}), bf16[1152,1664]{0,1:T(8,128)(2,1)}) %all-gather.6.cloned.1.call-update) | async-done | bytes 3833872 | tf_op jit(solution)/shard_map/all_gather | solution.py:114
  186.4 2.8 fusion.114
  191.0 5.7 %all-to-all-start = ((f32[16,1,4640]{2,1,0:T(1,128)}), f32[16,1,4640]{2,1,0:T(1,128)S(1)}, u32[]{:S(2)}, u32[]{:S(2)}) async-start(f32[16,1,4640]{2,1,0:T(1,128)} %broadcast_in_dim.94), calls=%async_computation | async-start | bytes 606208 | tf_op jit(solution)/shard_map/all_to_all | solution.py:26
  197.5 5.9 %all-to-all-done = f32[16,1,4640]{2,1,0:T(1,128)S(1)} async-done(((f32[16,1,4640]{2,1,0:T(1,128)}), f32[16,1,4640]{2,1,0:T(1,128)S(1)}, u32[]{:S(2)}, u32[]{:S(2)}) %all-to-all-start) | async-done | bytes 296992 | tf_op jit(solution)/shard_map/all_to_all | solution.py:26
  204.9 10.0 %scatter_custom_fusion = bf16[1153,104]{1,0:T(8,128)(2,1)S(1)} fusion(s32[2304]{0:T(1024)S(1)} %fusion.68, bf16[2304,104]{1,0:T(8,128)(2,1)S(1)} %bitcast.72, bf16[]{:T(256)} %constant.60.clone.1), kind=kCustom, calls=%fused_computation.95 | custom fusion | bytes 239826 | tf_op jit(solution)/shard_map/scatter | solution.py:143
  215.0 37.8 %all_to_all.21 = bf16[32,36,104]{2,1,0:T(8,128)(2,1)S(1)} all-to-all(bf16[32,36,104]{2,1,0:T(8,128)(2,1)S(1)} %reshape.294), channel_id=1, replica_groups=mesh['dp_0'=4,'dp_1'=4,'expert'=32] {'expert'}, dimensions={0} | all-to-all | bytes 479232 | tf_op jit(solution)/shard_map/all_to_all | solution.py:146
  253.9 54.4 %all-gather.8.cloned.1.call-done = bf16[1152,1664]{0,1:T(8,128)(2,1)} async-done(((bf16[1152,104]{0,1:T(8,128)(2,1)}), bf16[1152,1664]{0,1:T(8,128)(2,1)}) %all-gather.8.cloned.1.call-update) | async-done | bytes 3833872 | tf_op jit(solution)/shard_map/all_gather | solution.py:150
  308.2 13.8 %fusion = bf16[1664,1152]{0,1:T(8,128)(2,1)} fusion(bf16[1,512,1664]{2,1,0:T(8,128)(2,1)S(1)} %copy-done, bf16[1152,1664]{0,1:T(8,128)(2,1)} %all-gather.8.cloned.1.call-done, bf16[1,1664,512]{2,1,0:T(8,128)(2,1)} %param.20), kind=kOutput, calls=%fused_computation.5 | convolution fusion | flops 3966124032 | bytes 11075584 | tf_op jit(solution)/shard_map/hf,sh->fs/dot_general | solution.py:156
  322.0 6.4 %copy.86 = bf16[1664,1152]{1,0:T(8,128)(2,1)} copy(bf16[1664,1152]{0,1:T(8,128)(2,1)} %fusion) | data formatting | bytes 7667712 | tf_op jit(solution)/shard_map/convert_element_type | solution.py:156
  328.4 5.7 %all-to-all-start.2 = ((bf16[16,104,1152]{2,1,0:T(8,128)(2,1)}), bf16[16,104,1152]{2,1,0:T(8,128)(2,1)}, u32[]{:S(2)}, u32[]{:S(2)}) async-start(bf16[16,104,1152]{2,1,0:T(8,128)(2,1)} %bitcast.67), calls=%async_computation.2 | async-start | bytes 7667712 | tf_op jit(solution)/shard_map/all_to_all | solution.py:50
  335.7 54.6 %all-to-all-done.2 = bf16[16,104,1152]{2,1,0:T(8,128)(2,1)} async-done(((bf16[16,104,1152]{2,1,0:T(8,128)(2,1)}), bf16[16,104,1152]{2,1,0:T(8,128)(2,1)}, u32[]{:S(2)}, u32[]{:S(2)}) %all-to-all-start.2) | async-done | bytes 3833888 | tf_op jit(solution)/shard_map/all_to_all | solution.py:50
  390.3 2.7 reduce_sum.100
  394.1 12.8 %all-to-all-start.3 = ((bf16[104,32,36]{0,2,1:T(8,128)(2,1)}), bf16[104,32,36]{0,2,1:T(8,128)(2,1)S(1)}, u32[]{:S(2)}, u32[]{:S(2)}) async-start(bf16[104,32,36]{0,2,1:T(8,128)(2,1)} %reshape.297), calls=%async_computation.3 | async-start | bytes 655360 | tf_op jit(solution)/shard_map/all_to_all | solution.py:163
  408.4 23.8 %all-to-all-done.3 = bf16[104,32,36]{0,2,1:T(8,128)(2,1)S(1)} async-done(((bf16[104,32,36]{0,2,1:T(8,128)(2,1)}), bf16[104,32,36]{0,2,1:T(8,128)(2,1)S(1)}, u32[]{:S(2)}, u32[]{:S(2)}) %all-to-all-start.3) | async-done | bytes 239648 | tf_op jit(solution)/shard_map/all_to_all | solution.py:163
  432.3 6.0 %gather_fusion.1 = bf16[2304,104]{1,0:T(8,128)(2,1)} fusion(bf16[104,1152]{0,1:T(8,128)(2,1)S(1)} %reshape.298, s32[3072]{0:T(1024)} %pad_clamp_fusion), kind=kCustom, calls=%fused_computation.1 | custom fusion | bytes 967680 | tf_op jit(solution)/shard_map/jit(_take)/gather | solution.py:166
  438.3 7.9 %multiply_reduce_fusion = f32[104,1152]{0,1:T(8,128)S(1)} fusion(bf16[104,1152,2]{0,2,1:T(2,128)(2,1)} %bitcast.70, pred[1152,2]{1,0:T(8,128)(4,1)S(1)} %copy.80, f32[1152,2]{1,0:T(8,128)S(1)} %copy.90), kind=kLoop, calls=%fused_computation.34 | loop fusion | flops 838656 | bytes 969984 | tf_op jit(solution)/shard_map/reduce_sum | solution.py:169
  447.5 10.2 %scatter_custom_fusion.1 = f32[1489,104]{1,0:T(8,128)S(1)} fusion(s32[1152]{0:T(1024)} %get-tuple-element.10, f32[1152,104]{1,0:T(8,128)} %copy.92, f32[]{:T(128)} %constant.46.clone.1), kind=kCustom, calls=%fused_computation.81 | custom fusion | flops 119808 | bytes 619936 | tf_op jit(solution)/shard_map/scatter-add | solution.py:173
  457.8 6.2 %collective-permute-done.1 = bf16[31,24,104]{2,1,0:T(8,128)(2,1)S(1)} collective-permute-done((bf16[31,24,104]{2,1,0:T(8,128)(2,1)S(1)}, bf16[31,24,104]{2,1,0:T(8,128)(2,1)S(1)}, u32[]{:S(2)}, u32[]{:S(2)}) %collective-permute-start.1) | collective-permute-done | bytes 154784 | tf_op jit(solution)/shard_map/ppermute | solution.py:15
  (103 shorter events, 19.8 us)
Async XLA Ops:
  6.5 301.7 %copy-start = (bf16[1,512,1664]{2,1,0:T(8,128)(2,1)S(1)}, bf16[1,512,1664]{2,1,0:T(8,128)(2,1)}, u32[]{:S(2)}) copy-start(bf16[1,512,1664]{2,1,0:T(8,128)(2,1)} %param.21) | copy-start | bytes 5111812
  6.5 47.4 %copy-start.13 = (f32[104]{0:T(128)S(1)}, f32[104]{0:T(128)}, u32[]{:S(2)}) copy-start(f32[104]{0:T(128)} %param.15) | copy-start | bytes 1252
  6.5 107.4 %all-gather.4.cloned.1.call-start = ((), (), s32[]{:S(2)}) async-start(), calls=%async_computation.4 | async-start | bytes 4073472 | tf_op jit(solution)/shard_map/all_gather | solution.py:99
  6.5 12.4 %collective-permute-start = (bf16[31,24,104]{2,1,0:T(8,128)(2,1)}, bf16[31,24,104]{2,1,0:T(8,128)(2,1)S(1)}, u32[]{:S(2)}, u32[]{:S(2)}) collective-permute-start(bf16[31,24,104]{2,1,0:T(8,128)(2,1)} %param.12), channel_id=1, source_target_pairs={{1,0},{2,1},{3,2},{4,3},{5,4},{6,5},{7,6},{8,7},{9,8},{10,9},{11,1... | collective-permute-start | bytes 464264 | tf_op jit(solution)/shard_map/ppermute | solution.py:15
  54.8 131.7 %all-gather.6.cloned.1.call-start = ((), (), s32[]{:S(2)}) async-start(), calls=%async_computation.5 | async-start | bytes 4073472 | tf_op jit(solution)/shard_map/all_gather | solution.py:114
  119.6 1.9 copy-start.11
  119.6 1.8 copy-start.12
  119.7 66.8 %copy-start.1 = (bf16[1664,104]{0,1:T(8,128)(2,1)S(1)}, bf16[1664,104]{0,1:T(8,128)(2,1)}, u32[]{:S(2)}) copy-start(bf16[1664,104]{0,1:T(8,128)(2,1)} %param.17) | copy-start | bytes 1038340
  121.6 67.9 %copy-start.2 = (s32[1152,2]{0,1:T(2,128)S(1)}, s32[1152,2]{0,1:T(2,128)}, u32[]{:S(2)}) copy-start(s32[1152,2]{0,1:T(2,128)} %param.22) | copy-start | bytes 27652
  189.3 7.5 %copy-start.5 = (s32[1152,2]{0,1:T(2,128)S(1)}, s32[1152,2]{0,1:T(2,128)}, u32[]{:S(2)}) copy-start(s32[1152,2]{0,1:T(2,128)} %param.23) | copy-start | bytes 27652
  191.0 12.4 %all-to-all-start = ((f32[16,1,4640]{2,1,0:T(1,128)}), f32[16,1,4640]{2,1,0:T(1,128)S(1)}, u32[]{:S(2)}, u32[]{:S(2)}) async-start(f32[16,1,4640]{2,1,0:T(1,128)} %broadcast_in_dim.94), calls=%async_computation | async-start | bytes 606208 | tf_op jit(solution)/shard_map/all_to_all | solution.py:26
  196.7 111.5 %all-gather.8.cloned.1.call-start = ((), (), s32[]{:S(2)}) async-start(), calls=%async_computation.6 | async-start | bytes 4073472 | tf_op jit(solution)/shard_map/all_gather | solution.py:150
  203.6 132.1 %copy-start.3 = (f32[4640]{0:T(1024)}, f32[4640]{0:T(1024)S(1)}, u32[]{:S(2)}) copy-start(f32[4640]{0:T(1024)S(1)} %reduce_sum.99) | copy-start | bytes 55684
  203.6 0.6 copy-start.7
  203.7 0.6 copy-start.9
  328.4 62.0 %all-to-all-start.2 = ((bf16[16,104,1152]{2,1,0:T(8,128)(2,1)}), bf16[16,104,1152]{2,1,0:T(8,128)(2,1)}, u32[]{:S(2)}, u32[]{:S(2)}) async-start(bf16[16,104,1152]{2,1,0:T(8,128)(2,1)} %bitcast.67), calls=%async_computation.2 | async-start | bytes 7667712 | tf_op jit(solution)/shard_map/all_to_all | solution.py:50
  335.7 71.3 %copy-start.4 = (f32[4640]{0:T(1024)S(1)}, f32[4640]{0:T(1024)}, u32[]{:S(2)}) copy-start(f32[4640]{0:T(1024)} %copy-done.3) | copy-start | bytes 55684
  393.0 14.8 %copy-start.8 = (f32[1152]{0:T(1024)S(1)}, f32[1152]{0:T(1024)}, u32[]{:S(2)}) copy-start(f32[1152]{0:T(1024)} %copy-done.7) | copy-start | bytes 13828
  393.1 14.7 %copy-start.10 = (f32[1152]{0:T(1024)S(1)}, f32[1152]{0:T(1024)}, u32[]{:S(2)}) copy-start(f32[1152]{0:T(1024)} %copy-done.9) | copy-start | bytes 13828
  393.1 15.0 %copy-start.6 = (s32[1152,2]{0,1:T(2,128)S(1)}, s32[1152,2]{0,1:T(2,128)}, u32[]{:S(2)}) copy-start(s32[1152,2]{0,1:T(2,128)} %param.23) | copy-start | bytes 27652
  394.1 38.0 %all-to-all-start.3 = ((bf16[104,32,36]{0,2,1:T(8,128)(2,1)}), bf16[104,32,36]{0,2,1:T(8,128)(2,1)S(1)}, u32[]{:S(2)}, u32[]{:S(2)}) async-start(bf16[104,32,36]{0,2,1:T(8,128)(2,1)} %reshape.297), calls=%async_computation.3 | async-start | bytes 655360 | tf_op jit(solution)/shard_map/all_to_all | solution.py:163
  457.8 6.3 %collective-permute-start.1 = (bf16[31,24,104]{2,1,0:T(8,128)(2,1)S(1)}, bf16[31,24,104]{2,1,0:T(8,128)(2,1)S(1)}, u32[]{:S(2)}, u32[]{:S(2)}) collective-permute-start(bf16[31,24,104]{2,1,0:T(8,128)(2,1)S(1)} %slice.95), channel_id=1, source_target_pairs={{31,0},{0,1},{1,2},{2,3},{3,4},{4,5},{5,6},{6,7},{7,8},{8,9},{9,10... | collective-permute-start | bytes 464264 | tf_op jit(solution)/shard_map/ppermute | solution.py:15
Sparse Core Ops, SparseCore 0:
  54.9 58.9 all-gather.3
  121.6 64.7 all-gather.5
  254.0 54.2 all-gather.7
where the time goes:
time: 472 us; the launch traced here: 471 us
  waiting for transfers between devices  270 us (57%)
  blocking collectives  68.6 us (15%)
  local copies, waits for them, and re-layouts  37.7 us (8%)
  starting transfers between devices  33.3 us (7%)
  other arithmetic  25.5 us (5%)
  matrix products  22.3 us (5%)
  between operations  14.2 us (3%)
    all_gather x1, waiting for transfers between devices, body(): lax.all_gather(attended, DP, axis=1, tiled=True)  64.8 us
    all_gather x1, waiting for transfers between devices, body(): lax.all_gather(normed, DP, axis=1, tiled=True)  59.1 us
    all_to_all x1, waiting for transfers between devices, sum_at_owner(): pieces = lax.all_to_all(in_blocks(x, dim, length), axis, 0, 0, tiled=True)  54.6 us
    all_gather x1, waiting for transfers between devices, body(): lax.all_gather(slot_rows, DP, axis=1, tiled=True)  54.4 us
    all_to_all x1, blocking collectives, body(): lax.all_to_all(outbound, 'expert', split_axis=0, concat_axis=0, tiled=True)  37.8 us
    psum x2, blocking collectives, by_axis(): x = lax.psum(x, axis)  30.8 us
    all_to_all x1, waiting for transfers between devices, body(): lax.all_to_all(returned, 'expert', split_axis=1, concat_axis=1, tiled=True)  23.8 us
    dot_general x1, matrix products, body(): jnp.einsum('hf,sh->fs', second_layer, activated, preferred_element_type=j...  13.8 us
  transfers between devices with their start and end apart: 8, of which 8 were waited for; matrix products, arithmetic and copies ran while one was open for 1% of the time, Pallas kernels for 0%

commit v1 on v0

v1 whole, which is shorter than its diff:
```python
import functools

import jax
import jax.numpy as jnp
from jax import lax
from jax.experimental import pallas as pl
from jax.experimental.pallas import tpu as pltpu
from jax.sharding import Mesh
from jax.sharding import PartitionSpec as P

HEAD_DIM = 104
TILE_SIDE = 24
SIDE = 4
SPAN = 7
DP = ("y", "x")
MESH = pl.DeviceIdType.MESH
BF16 = jnp.bfloat16
F32 = jnp.float32
STEPS = (0, -1, 1, 2)


def near(axis, distance):
    return lax.rem(lax.axis_index(axis) + distance + SIDE, SIDE)


def block_at(primary, along, across):
    if primary == "x":
        return near("y", across) * SIDE + near("x", along)
    return near("y", along) * SIDE + near("x", across)


def greet_neighbours():
    barrier = pltpu.get_barrier_semaphore()
    for axis in DP:
        for step in (1, -1):
            pl.semaphore_signal(
                barrier, inc=1, device_id={axis: near(axis, step)}, device_id_type=MESH
            )
    pl.semaphore_wait(barrier, 4)


def chunks_of(lanes):
    first = (lanes // 128 + 1) // 2 * 128
    return (("x", "y", pl.ds(0, first)), ("y", "x", pl.ds(first, lanes - first)))


def row_halves(rows):
    low = rows // 2 // 16 * 16
    return (pl.ds(0, low), pl.ds(low, rows - low))


def gather_kernel(x_ref, out_ref, local_sem, send_sem, recv_sem):
    rows, lanes = x_ref.shape
    chunks = chunks_of(lanes)
    halves = row_halves(rows)
    own = pltpu.make_async_copy(x_ref, out_ref.at[block_at("x", 0, 0)], local_sem)
    own.start()
    greet_neighbours()
    own.wait()
    sent = []

    def copy_of(c, group, way, step, along, across):
        primary, secondary, span = chunks[c]
        axis = primary if group == 0 else secondary
        part = pl.ds(0, rows) if step == 0 else halves[way ^ c]
        ref = out_ref.at[block_at(primary, along, across), part, span]
        return pltpu.make_async_remote_copy(
            src_ref=ref,
            dst_ref=ref,
            send_sem=send_sem.at[c, group, way, step],
            recv_sem=recv_sem.at[c, group, way, step],
            device_id={axis: near(axis, 1 - 2 * way)},
            device_id_type=MESH,
        )

    def send(*which):
        copy = copy_of(*which)
        copy.start()
        sent.append(copy)

    def arrive(*which):
        copy_of(*which).wait_recv()

    for c in (0, 1):
        for way in (0, 1):
            send(c, 0, way, 0, 0, 0)
    for c in (0, 1):
        for way in (0, 1):
            send(c, 1, way, 0, 0, 0)
    for way in (0, 1):
        for c in (0, 1):
            back = 2 * way - 1
            arrive(c, 0, way, 0, back, 0)
            send(c, 0, way, 1, back, 0)
            for turn in (0, 1):
                send(c, 2 + way, turn, 0, back, 0)
    for way in (0, 1):
        for c in (0, 1):
            back = 2 * way - 1
            arrive(c, 1, way, 0, 0, back)
            send(c, 1, way, 1, 0, back)
    for c in (0, 1):
        for way in (0, 1):
            arrive(c, 0, way, 1, 2, 0)
        for turn in (0, 1):
            send(c, 4, turn, 0, 2, 0)
    for group in (2, 3, 4):
        for way in (0, 1):
            for c in (0, 1):
                along = STEPS[group - 1]
                back = 2 * way - 1
                arrive(c, group, way, 0, along, back)
                send(c, group, way, 1, along, back)
    for group in (1, 2, 3, 4):
        for way in (0, 1):
            for c in (0, 1):
                arrive(c, group, way, 1, STEPS[group - 1], 2)
    for copy in sent:
        copy.wait_send()


def from_group(x, ident):
    rows, lanes = x.shape
    return pl.pallas_call(
        gather_kernel,
        out_shape=jax.ShapeDtypeStruct((SIDE * SIDE, rows, lanes), x.dtype),
        in_specs=[pl.BlockSpec(memory_space=pl.ANY)],
        out_specs=pl.BlockSpec(memory_space=pltpu.VMEM),
        scratch_shapes=[
            pltpu.SemaphoreType.DMA,
            pltpu.SemaphoreType.DMA((2, 5, 2, 2)),
            pltpu.SemaphoreType.DMA((2, 5, 2, 2)),
        ],
        compiler_params=pltpu.CompilerParams(
            collective_id=ident, has_side_effects=True, vmem_limit_bytes=48 << 20
        ),
        name=f"gather_{ident}",
    )(x)


def reduce_kernel(part_ref, out_ref, mid_ref, sum_ref, in_ref, red_ref, send_sem, recv_sem):
    blocks, rows, lanes = part_ref.shape
    chunks = chunks_of(lanes)
    halves = row_halves(rows)
    sent = []
    greet_neighbours()

    def own_ref(c, group, along, across):
        primary, _, span = chunks[c]
        if group:
            return part_ref.at[block_at(primary, along, across), :, span]
        return red_ref.at[c, STEPS.index(along), :, pl.ds(0, span.size)]

    def copy_of(c, group, way, step, src):
        primary, secondary, span = chunks[c]
        axis = secondary if group else primary
        half = halves[way] if step != 1 else halves[1 - way]
        width = pl.ds(0, span.size)
        if step == 0:
            dst = mid_ref.at[c, group, way, pl.ds(0, half.size), width]
        else:
            dst = in_ref.at[c, group, way, half, width]
        return pltpu.make_async_remote_copy(
            src_ref=dst if src is None else src,
            dst_ref=dst,
            send_sem=send_sem.at[c, group, way, step],
            recv_sem=recv_sem.at[c, group, way, step],
            device_id={axis: near(axis, 1 - 2 * way)},
            device_id_type=MESH,
        )

    def send(c, group, way, step, src):
        copy = copy_of(c, group, way, step, src)
        copy.start()
        sent.append(copy)

    def block(c, group, along_step):
        if group:
            return own_ref(c, group, STEPS[group - 1], along_step)
        return own_ref(c, group, along_step, 0)

    def first_part(c, group):
        for way in (0, 1):
            send(c, group, way, 0, block(c, group, 2).at[halves[way]])
        for way in (0, 1):
            send(c, group, way, 1, block(c, group, 1 - 2 * way).at[halves[1 - way]])

    def second_part(c, group):
        width = pl.ds(0, chunks[c][2].size)
        for way in (0, 1):
            half = halves[way]
            size = pl.ds(0, half.size)
            copy_of(c, group, way, 0, None).wait_recv()
            mine = block(c, group, 1 - 2 * way)[half, :].astype(F32)
            sum_ref[c, group, way, size, width] = (
                mine + mid_ref[c, group, way, size, width].astype(F32)
            ).astype(sum_ref.dtype)
            send(c, group, way, 2, sum_ref.at[c, group, way, size, width])

    def total(c, group):
        width = pl.ds(0, chunks[c][2].size)
        for way in (0, 1):
            copy_of(c, group, way, 1, None).wait_recv()
            copy_of(c, group, way, 2, None).wait_recv()
        mine = block(c, group, 0)[...].astype(F32)
        return (
            mine
            + in_ref[c, group, 0, :, width].astype(F32)
            + in_ref[c, group, 1, :, width].astype(F32)
        )

    order = (4, 2, 3, 1)
    for group in order:
        for c in (0, 1):
            first_part(c, group)
    for group in order:
        for c in (0, 1):
            second_part(c, group)
    for group in order:
        for c in (0, 1):
            red_ref[c, group - 1, :, pl.ds(0, chunks[c][2].size)] = total(c, group).astype(
                red_ref.dtype
            )
            if group == 4:
                for way in (0, 1):
                    send(c, 0, way, 0, block(c, 0, 2).at[halves[way]])
            elif group != 1:
                way = 0 if group == 3 else 1
                send(c, 0, way, 1, block(c, 0, 1 - 2 * way).at[halves[1 - way]])
    for c in (0, 1):
        second_part(c, 0)
    for c in (0, 1):
        out_ref[:, chunks[c][2]] = total(c, 0).astype(out_ref.dtype)
    for copy in sent:
        copy.wait_send()


def sum_at_owner(part, ident):
    blocks, rows, lanes = part.shape
    widest = chunks_of(lanes)[0][2].size
    half = row_halves(rows)[1].size
    return pl.pallas_call(
        reduce_kernel,
        out_shape=jax.ShapeDtypeStruct((rows, lanes), part.dtype),
        in_specs=[pl.BlockSpec(memory_space=pltpu.VMEM)],
        out_specs=pl.BlockSpec(memory_space=pltpu.VMEM),
        scratch_shapes=[
            pltpu.VMEM((2, 5, 2, half, widest), part.dtype),
            pltpu.VMEM((2, 5, 2, half, widest), part.dtype),
            pltpu.VMEM((2, 5, 2, rows, widest), part.dtype),
            pltpu.VMEM((2, 4, rows, widest), part.dtype),
            pltpu.SemaphoreType.DMA((2, 5, 2, 3)),
            pltpu.SemaphoreType.DMA((2, 5, 2, 3)),
        ],
        compiler_params=pltpu.CompilerParams(
            collective_id=ident, has_side_effects=True, vmem_limit_bytes=48 << 20
        ),
        name=f"reduce_{ident}",
    )(part)


def exchange_order(count):
    ring = count // 2
    return sorted(range(1, count), key=lambda d: -min(d // 2, ring - d // 2))


def exchange_kernel(x_ref, out_ref, local_sem, send_sem, recv_sem):
    count = x_ref.shape[0]
    me = lax.axis_index("expert")
    barrier = pltpu.get_barrier_semaphore()
    for d in range(1, count):
        pl.semaphore_signal(
            barrier,
            inc=1,
            device_id={"expert": lax.rem(me + d, count)},
            device_id_type=MESH,
        )
    own = pltpu.make_async_copy(x_ref.at[me], out_ref.at[me], local_sem)
    own.start()
    pl.semaphore_wait(barrier, count - 1)
    sent = []
    for d in exchange_order(count):
        peer = lax.rem(me + d, count)
        copy = pltpu.make_async_remote_copy(
            src_ref=x_ref.at[peer],
            dst_ref=out_ref.at[me],
            send_sem=send_sem.at[d],
            recv_sem=recv_sem.at[d],
            device_id={"expert": peer},
            device_id_type=MESH,
        )
        copy.start()
        sent.append(copy)
    own.wait()
    for d in exchange_order(count):
        source = lax.rem(me - d + count, count)
        pltpu.make_async_remote_copy(
            src_ref=x_ref.at[source],
            dst_ref=out_ref.at[source],
            send_sem=send_sem.at[d],
            recv_sem=recv_sem.at[d],
            device_id={"expert": source},
            device_id_type=MESH,
        ).wait_recv()
    for copy in sent:
        copy.wait_send()


def exchanged(x, ident):
    count = x.shape[0]
    return pl.pallas_call(
        exchange_kernel,
        out_shape=jax.ShapeDtypeStruct(x.shape, x.dtype),
        in_specs=[pl.BlockSpec(memory_space=pltpu.VMEM)],
        out_specs=pl.BlockSpec(memory_space=pltpu.VMEM),
        scratch_shapes=[
            pltpu.SemaphoreType.DMA,
            pltpu.SemaphoreType.DMA((count,)),
            pltpu.SemaphoreType.DMA((count,)),
        ],
        compiler_params=pltpu.CompilerParams(collective_id=ident, has_side_effects=True),
        name=f"exchange_{ident}",
    )(x)


def sums_kernel(x_ref, out_ref, mid_ref, in_ref, send_sem, recv_sem):
    barrier = pltpu.get_barrier_semaphore()
    for axis in DP:
        for d in (1, 2, 3):
            pl.semaphore_signal(
                barrier, inc=1, device_id={axis: near(axis, d)}, device_id_type=MESH
            )
    pl.semaphore_wait(barrier, 6)
    for phase, axis in enumerate(("x", "y")):
        src = x_ref if phase == 0 else mid_ref
        copies = []
        for d in (2, 1, 3):
            copy = pltpu.make_async_remote_copy(
                src_ref=src,
                dst_ref=in_ref.at[phase, d],
                send_sem=send_sem.at[phase, d],
                recv_sem=recv_sem.at[phase, d],
                device_id={axis: near(axis, d)},
                device_id_type=MESH,
            )
            copy.start()
            copies.append(copy)
        for copy in copies:
            copy.wait()
        result = src[...] + in_ref[phase, 1] + in_ref[phase, 2] + in_ref[phase, 3]
        if phase == 0:
            mid_ref[...] = result
        else:
            out_ref[...] = result


def summed(x, ident):
    return pl.pallas_call(
        sums_kernel,
        out_shape=jax.ShapeDtypeStruct(x.shape, x.dtype),
        in_specs=[pl.BlockSpec(memory_space=pltpu.VMEM)],
        out_specs=pl.BlockSpec(memory_space=pltpu.VMEM),
        scratch_shapes=[
            pltpu.VMEM(x.shape, x.dtype),
            pltpu.VMEM((2, 4, *x.shape), x.dtype),
            pltpu.SemaphoreType.DMA((2, 4)),
            pltpu.SemaphoreType.DMA((2, 4)),
        ],
        compiler_params=pltpu.CompilerParams(collective_id=ident, has_side_effects=True),
        name=f"sums_{ident}",
    )(x)


def passed_along(block, axis, distance):
    size = lax.axis_size(axis)
    return lax.ppermute(block, axis, [((i - distance) % size, i) for i in range(size)])


def two_parts(x):
    high = x.astype(BF16)
    return high, (x - high.astype(F32)).astype(BF16)


def three_parts(x):
    high, rest = x.astype(BF16), x
    rest = x - high.astype(F32)
    middle = rest.astype(BF16)
    return high, middle, (rest - middle.astype(F32)).astype(BF16)


def body(
    panorama,
    tile_anchor,
    tile_count,
    pre_attention_gain,
    qkv_weight,
    out_weight,
    pre_expert_gain,
    router_weight,
    expand_weight,
    reduce_weight,
    route_index,
    slot_index,
):
    expert_count = lax.axis_size("expert")
    height, own_width, features = panorama.shape
    group = SIDE * SIDE
    full_width = features * group
    tiles_here = tile_anchor.shape[0]
    tile_tokens = TILE_SIDE * TILE_SIDE
    column_tokens = tiles_here * tile_tokens
    experts = router_weight.shape[1]
    capacity = column_tokens // experts
    stride = (capacity + 7) // 8 * 8
    own_patches = height * own_width
    own_lanes = (own_patches + 3 + 127) // 128 * 128
    side_patches = height * SPAN
    side_lanes = (side_patches + 127) // 128 * 128

    across = jnp.transpose(panorama, (2, 1, 0)).reshape(features, own_patches)
    gain_columns = jnp.stack(three_parts(pre_attention_gain), axis=1)
    sent = jnp.concatenate(
        [across, gain_columns, jnp.zeros((features, own_lanes - own_patches - 3), BF16)], axis=1
    )
    side_raw = passed_along(across[:, :side_patches], "expert", -1)
    raw = from_group(sent, 1).reshape(full_width, own_lanes)
    raw32 = raw.astype(F32)
    gain = jnp.sum(raw32[:, own_patches : own_patches + 3], axis=1, keepdims=True)
    mean_value = jnp.sum(raw32, axis=0, keepdims=True) / full_width
    square_value = jnp.sum(raw32 * raw32, axis=0, keepdims=True) / full_width
    inverse_std = lax.rsqrt(square_value - mean_value * mean_value + 1e-06)
    normed = ((raw32 - mean_value) * inverse_std * gain).astype(BF16)
    projected = jnp.einsum("sfo,ft->sot", qkv_weight, normed, preferred_element_type=F32).astype(
        BF16
    )
    side = passed_along(projected[:, :, :side_patches], "expert", -1)
    pad = ((0, 0), (0, 0), (0, side_lanes - side_patches))
    area = jnp.concatenate([projected, jnp.pad(side, pad)], axis=2)
    raw_area = jnp.concatenate([sent, jnp.pad(side_raw, pad[1:])], axis=1)

    step_ids = jnp.arange(tile_tokens, dtype=jnp.int32)
    patch_rows = tile_anchor[:, 0:1] + (step_ids // TILE_SIDE)[None, :]
    patch_cols = tile_anchor[:, 1:2] + (step_ids % TILE_SIDE)[None, :]
    flat = jnp.where(
        patch_cols < own_width,
        patch_cols * height + patch_rows,
        own_lanes + (patch_cols - own_width) * height + patch_rows,
    ).reshape(column_tokens)
    live_tile = jnp.arange(tiles_here, dtype=jnp.int32) < tile_count[0]
    live = jnp.repeat(live_tile, tile_tokens)
    area_ids = jnp.arange(own_lanes + side_lanes, dtype=jnp.int32)
    chosen_patch = (area_ids[:, None] == flat[None, :]).astype(BF16)

    tokens = jnp.dot(raw_area, chosen_patch, preferred_element_type=F32)
    shaped = jnp.einsum("sop,pn->son", area, chosen_patch, preferred_element_type=F32).astype(BF16)
    shaped = shaped.reshape(3, features, tiles_here, tile_tokens)
    scores = jnp.einsum(
        "daq,dak->aqk", shaped[0], shaped[1], preferred_element_type=F32
    ) * HEAD_DIM ** (-0.5)
    weights = jnp.exp(scores)
    weights = (weights / jnp.sum(weights, axis=-1, keepdims=True)).astype(BF16)
    attended = jnp.einsum("dak,aqk->daq", shaped[2], weights, preferred_element_type=F32)
    attended = attended.astype(BF16).reshape(features, column_tokens)
    everyone = from_group(attended, 2).reshape(full_width, column_tokens)
    mixed = tokens + jnp.einsum("fo,fn->on", out_weight, everyone, preferred_element_type=F32)

    route = route_index.T
    slot = slot_index.T
    expert_ids = jnp.arange(experts, dtype=jnp.int32)
    chosen = route[:, None, :] == expert_ids[None, :, None]

    def picked(table):
        return jnp.sum(jnp.where(chosen, table[None], 0.0), axis=1)

    router_rows = router_weight.T
    direct = jnp.dot(
        router_rows * pre_expert_gain[None, :], mixed, precision=lax.Precision.HIGHEST
    )
    gain_scores = jnp.sum(router_rows * pre_expert_gain[None, :], axis=1)
    partial = jnp.concatenate(
        [
            jnp.sum(mixed, axis=0, keepdims=True),
            jnp.sum(mixed * mixed, axis=0, keepdims=True),
            picked(direct),
        ],
        axis=0,
    ).reshape(4 * tiles_here, tile_tokens)
    extra = jnp.broadcast_to(
        jnp.pad(gain_scores, (0, 64 - experts))[None, :], (4 * tiles_here, 64)
    )
    totals = summed(jnp.concatenate([partial, extra], axis=1), 3)
    gain_sum = totals[0, tile_tokens : tile_tokens + experts]
    totals = totals[:, :tile_tokens].reshape(4, column_tokens)
    mean_value = totals[0:1] / full_width
    inverse_std = lax.rsqrt(totals[1:2] / full_width - mean_value * mean_value + 1e-06)
    expert_in = (mixed - mean_value) * inverse_std * pre_expert_gain[:, None]
    expert_in = jnp.where(live[None, :], expert_in, 0.0).astype(BF16)
    logits = inverse_std * (totals[2:4] - mean_value * picked(gain_sum[:, None]))
    gates = jax.nn.sigmoid(logits - logits[::-1])
    keep = slot >= 0
    target = jnp.where(keep, route * stride + slot, -1)
    slot_ids = jnp.arange(experts * stride, dtype=jnp.int32)
    hits = slot_ids[None, :, None] == target[:, None, :]
    chosen_slot = (hits[0] | hits[1]).astype(BF16)
    outbound = jnp.einsum("qn,fn->qf", chosen_slot, expert_in, preferred_element_type=F32)
    outbound = outbound.astype(BF16).reshape(experts, stride, features)
    inbound = exchanged(outbound, 4)
    slots = jnp.transpose(inbound[:, :capacity], (2, 0, 1)).reshape(
        features, expert_count * capacity
    )
    rows_in = from_group(slots, 5).reshape(full_width, expert_count * capacity)
    hidden_pre = jnp.einsum("fs,fh->sh", rows_in, expand_weight[0], preferred_element_type=F32)
    activated = jax.nn.gelu(hidden_pre, approximate=False).astype(BF16)
    partial_out = jnp.einsum(
        "hf,sh->fs", reduce_weight[0], activated, preferred_element_type=F32
    ).astype(BF16)
    expert_sum = sum_at_owner(
        partial_out.reshape(group, features, expert_count * capacity), 6
    )
    returned = jnp.transpose(
        expert_sum.reshape(features, expert_count, capacity), (1, 2, 0)
    )
    returned = jnp.pad(returned, ((0, 0), (0, stride - capacity), (0, 0)))
    fetched = exchanged(returned, 7).reshape(experts * stride, features)
    gates = jnp.where(keep & live[None, :], gates, 0.0)
    mixing = jnp.where(hits[0], gates[0:1], 0.0) + jnp.where(hits[1], gates[1:2], 0.0)
    final = mixed
    for piece in two_parts(mixing):
        final = final + jnp.einsum("qf,qn->fn", fetched, piece, preferred_element_type=F32)
    final = jnp.where(live[None, :], final, 0.0)
    accumulated = 0.0
    for piece in two_parts(final):
        accumulated = accumulated + jnp.einsum(
            "fn,pn->fp", piece, chosen_patch, preferred_element_type=F32
        )
    incoming = passed_along(
        accumulated[:, own_lanes : own_lanes + side_patches].astype(BF16), "expert", 1
    ).astype(F32)
    result = accumulated[:, :own_patches] + jnp.pad(
        incoming, ((0, 0), (0, own_patches - side_patches))
    )
    result = result.astype(BF16).reshape(features, own_width, height)
    return jnp.transpose(result, (2, 1, 0))


def solution(mesh):
    split = Mesh(mesh.devices.reshape(SIDE, SIDE, mesh.shape["expert"]), ("y", "x", "expert"))
    return jax.shard_map(
        body,
        mesh=split,
        in_specs=(
            P(None, "expert", DP),
            P("expert", None),
            P("expert"),
            P(DP),
            P(None, None, DP),
            P(None, DP),
            P(DP),
            P(DP, None),
            P("expert", None, DP),
            P("expert", DP, None),
            P("expert", None),
            P("expert", None),
        ),
        out_specs=P(None, "expert", DP),
        check_vma=False,
    )
```

time: 472 us -> 244 us (0.52)
  waiting for transfers between devices: 270 us -> 4.62 us
  Pallas kernels: 0 us -> 167 us
  blocking collectives: 68.6 us -> 0 us
  starting transfers between devices: 33.3 us -> 9.13 us
  other arithmetic: 25.5 us -> 8.43 us
  local copies, waits for them, and re-layouts: 37.7 us -> 21.2 us
  between operations: 14.2 us -> 1.16 us
  matrix products: 22.3 us -> 31.5 us
    all_gather x3 -> x0, waiting for transfers between devices: 178 us -> none  [the longest x1 64.8 us: body(): lax.all_gather(attended, DP, axis=1, tiled=True)]
    pallas_call x0 -> x7, Pallas kernels: none -> 167 us  [the longest x3 76.9 us: from_group(): pl.pallas_call(gather_kernel, out_shape=jax.ShapeDtypeStruct((SIDE * SIDE...]
    all_to_all x3 -> x0, waiting for transfers between devices: 84.3 us -> none  [the longest x1 54.6 us: sum_at_owner(): pieces = lax.all_to_all(in_blocks(x, dim, length), axis, 0, 0, tiled=True)]
    all_to_all x1 -> x0, blocking collectives: 37.8 us -> none  [body(): lax.all_to_all(outbound, 'expert', split_axis=0, concat_axis=0, tiled=True)]
    psum x2 -> x0, blocking collectives: 30.8 us -> none  [by_axis(): x = lax.psum(x, axis)]
    all_to_all x3 -> x0, starting transfers between devices: 24.2 us -> none  [the longest x1 12.8 us: body(): lax.all_to_all(returned, 'expert', split_axis=1, concat_axis=1, tiled=True)]
    dot_general x6 -> x12, matrix products: 18.3 us -> 30.3 us  [the longest x1 13.7 us: body(): jnp.einsum('hf,sh->fs', reduce_weight[0], activated, preferred_element_ty...]
    scatter-add x1 -> x0, other arithmetic: 10.2 us -> none  [body(): jnp.zeros((height * 2 * own_width + 1, features), jnp.float32).at[out_index]]
  transfers between devices with their start and end apart: 8 -> 3, of which waited for: 8 -> 1; matrix products, arithmetic and copies ran while one was open for 1% -> 4% of each run, Pallas kernels for 0% -> 9%
where the time goes in v1:
time: 244 us; the launch traced here: 243 us
  Pallas kernels  167 us (68%)
  matrix products  31.5 us (13%)
  local copies, waits for them, and re-layouts  21.2 us (9%)
  starting transfers between devices  9.13 us (4%)
  other arithmetic  8.43 us (3%)
  waiting for transfers between devices  4.62 us (2%)
    pallas_call x3, Pallas kernels, from_group(): pl.pallas_call(gather_kernel, out_shape=jax.ShapeDtypeStruct((SIDE * SIDE...  76.9 us
    pallas_call x2, Pallas kernels, exchanged(): pl.pallas_call(exchange_kernel, out_shape=jax.ShapeDtypeStruct(x.shape, x...  51.6 us
    pallas_call x1, Pallas kernels, sum_at_owner(): pl.pallas_call(reduce_kernel, out_shape=jax.ShapeDtypeStruct((rows, lanes...  27.4 us
    dot_general x1, matrix products, body(): jnp.einsum('hf,sh->fs', reduce_weight[0], activated, preferred_element_ty...  13.7 us
    pallas_call x1, Pallas kernels, summed(): pl.pallas_call(sums_kernel, out_shape=jax.ShapeDtypeStruct(x.shape, x.dty...  10.8 us
    ppermute x3, starting transfers between devices, passed_along(): lax.ppermute(block, axis, [((i - distance) % size, i) for i in range(size)])  9.13 us
    dot_general x2, matrix products, body(): jnp.einsum('qf,qn->fn', fetched, piece, preferred_element_type=F32)  6.52 us
    convert_element_type x1, local copies, waits for them, and re-layouts, body(): partial_out = jnp.einsum('hf,sh->fs', reduce_weight[0], activated, prefer...  6.41 us
  transfers between devices with their start and end apart: 3, of which 1 were waited for; matrix products, arithmetic and copies ran while one was open for 4% of the time, Pallas kernels for 9%

profile of v1, /device:TPU:24, one launch (start us, length us, event | category | flops | bytes accessed | tf_op | source)
XLA Modules:
  0.0 242.6 jit_solution(9905316649506879374)
XLA Ops:
  0.0 1.1 copy.47
  1.2 8.9 %collective-permute-start = (bf16[104,217]{0,1:T(8,128)(2,1)S(1)}, bf16[104,217]{0,1:T(8,128)(2,1)S(1)}, u32[]{:S(2)}, u32[]{:S(2)}) collective-permute-start(bf16[104,217]{0,1:T(8,128)(2,1)S(1)} %slice.92), channel_id=1, source_target_pairs={{1,0},{2,1},{3,2},{4,3},{5,4},{6,5},{7,6},{8,7},{9,8},{10,9},{11,1... | collective-permute-start | bytes 135416 | tf_op jit(solution)/shard_map/ppermute | solution.py:376
  11.5 21.5 %gather_1.1 = bf16[16,104,768]{2,1,0:T(8,128)(2,1)S(1)} custom-call(bf16[104,768]{1,0:T(8,128)(2,1)S(1)} %concatenate.17.x_ref), custom_call_target="tpu_custom_call" | custom-call | tf_op jit(solution)/shard_map/gather_1/pallas_call | solution.py:124
  34.9 1.2 fusion.23
  36.5 4.0 %iota_compare_fusion = pred[2,1280,1152]{2,1,0:T(32,128)(4,1)} fusion(s32[2,1152]{1,0:T(2,128)S(1)} %fusion.116), kind=kLoop, calls=%fused_computation | loop fusion | flops 2949120 | bytes 2958336 | tf_op jit(solution)/shard_map/eq | solution.py:503
  42.3 1.2 fusion.19
  46.2 27.8 %gather_2.1 = bf16[16,104,1152]{2,1,0:T(8,128)(2,1)S(1)} custom-call(bf16[104,1152]{1,0:T(8,128)(2,1)S(1)} %reshape.198.x_ref), custom_call_target="tpu_custom_call" | custom-call | tf_op jit(solution)/shard_map/gather_2/pallas_call | solution.py:124
  74.8 1.0 fusion.162
  76.9 10.8 %sums_3.1 = f32[8,640]{1,0:T(8,128)} custom-call(f32[8,640]{1,0:T(8,128)} %pad_maximum_fusion.x_ref), custom_call_target="tpu_custom_call" | custom-call | tf_op jit(solution)/shard_map/sums_3/pallas_call | solution.py:358
  90.8 3.2 %fusion.37 = bf16[1280,104]{0,1:T(8,128)(2,1)S(1)} fusion(pred[2,1280,1152]{2,1,0:T(32,128)(4,1)} %iota_compare_fusion, f32[104,1152]{1,0:T(8,128)S(1)} %get-tuple-element.25, f32[104]{0:T(128)S(1)} %copy-done.10, f32[1152]{0:T(1024)S(1)} %add_rsqrt_fusion, f32[1152]{0:T(1024)S(1)} %div.43, pred[1152]{0:T(1024)(128)(4,1)S(1)} %broadcast_in_dim.106), kind=kOutput, calls=%fused_computation.38 | convolution fusion | flops 308915200 | bytes 3705376 | tf_op jit(solution)/shard_map/qn,fn->qf/dot_general | solution.py:505
  94.9 26.4 %exchange_4.1 = bf16[32,40,104]{2,1,0:T(8,128)(2,1)} custom-call(bf16[32,40,104]{2,1,0:T(8,128)(2,1)} %bitcast.99), custom_call_target="tpu_custom_call" | custom-call | tf_op jit(solution)/shard_map/exchange_4/pallas_call | solution.py:311
  121.3 1.0 slice_bitcast_fusion
  122.6 27.7 %gather_5.1 = bf16[16,104,1152]{2,1,0:T(8,128)(2,1)S(1)} custom-call(bf16[104,1152]{1,0:T(8,128)(2,1)S(1)} %copy.59.x_ref), custom_call_target="tpu_custom_call" | custom-call | tf_op jit(solution)/shard_map/gather_5/pallas_call | solution.py:124
  150.3 1.9 copy-done.2
  152.2 13.7 %fusion = bf16[1664,1152]{0,1:T(8,128)(2,1)} fusion(bf16[1,512,1664]{2,1,0:T(8,128)(2,1)S(1)} %copy-done, bf16[1664,1152]{1,0:T(8,128)(2,1)} %bitcast.97, bf16[1,1664,512]{2,1,0:T(8,128)(2,1)} %param.20), kind=kOutput, calls=%fused_computation.2 | convolution fusion | flops 3966124032 | bytes 11075584 | tf_op jit(solution)/shard_map/hf,sh->fs/dot_general | solution.py:514
  165.9 6.4 %copy.60 = bf16[1664,1152]{1,0:T(8,128)(2,1)} copy(bf16[1664,1152]{0,1:T(8,128)(2,1)} %fusion) | data formatting | bytes 7667712 | tf_op jit(solution)/shard_map/convert_element_type | solution.py:516
  172.3 2.1 copy-done.1
  174.4 27.4 %reduce_6.1 = bf16[104,1152]{1,0:T(8,128)(2,1)S(1)} custom-call(bf16[16,104,1152]{2,1,0:T(8,128)(2,1)S(1)} %bitcast.96), custom_call_target="tpu_custom_call" | custom-call | tf_op jit(solution)/shard_map/reduce_6/pallas_call | solution.py:242
  202.9 25.2 %exchange_7.1 = bf16[32,40,104]{2,1,0:T(8,128)(2,1)} custom-call(bf16[32,40,104]{2,1,0:T(8,128)(2,1)} %pad.26.x_ref), custom_call_target="tpu_custom_call" | custom-call | tf_op jit(solution)/shard_map/exchange_7/pallas_call | solution.py:311
  228.1 3.9 %fusion.17 = f32[104,1152]{1,0:T(8,128)S(1)} fusion(bf16[1280,104]{1,0:T(8,128)(2,1)} %bitcast.102, pred[2,1280,1152]{2,1,0:T(32,128)(4,1)} %iota_compare_fusion, f32[1152]{0:T(1024)S(1)} %get-tuple-element.10, f32[1152]{0:T(1024)S(1)} %get-tuple-element.9), kind=kOutput, calls=%fused_computation.25 | convolution fusion | flops 317030400 | bytes 3703808 | tf_op jit(solution)/shard_map/qf,qn->fn/dot_general | solution.py:529
  232.0 2.6 %fusion.34 = f32[104,1152]{1,0:T(8,128)S(1)} fusion(f32[104,1152]{1,0:T(8,128)S(1)} %fusion.17, f32[104,1152]{1,0:T(8,128)S(1)} %get-tuple-element.25, bf16[1280,104]{1,0:T(8,128)(2,1)S(1)} %bitcast.103, pred[2,1280,1152]{2,1,0:T(32,128)(4,1)S(1)} %copy-done.3, f32[1152]{0:T(1024)S(1)} %get-tuple-element.10, f32[1152]{0:T(1024)S(1)} %get-tuple-element.9, ...), kind=kOutput, calls=%fused_computation.36 | convolution fusion | flops 312966144 | bytes 4663424 | tf_op jit(solution)/shard_map/qf,qn->fn/dot_general | solution.py:529
  234.6 1.1 fusion.5
  235.7 1.1 fusion.61
  237.0 4.6 %collective-permute-done.2 = bf16[104,217]{1,0:T(8,128)(2,1)S(1)} collective-permute-done((bf16[104,217]{1,0:T(8,128)(2,1)S(1)}, bf16[104,217]{1,0:T(8,128)(2,1)S(1)}, u32[]{:S(2)}, u32[]{:S(2)}) %collective-permute-start.2) | collective-permute-done | bytes 45168 | tf_op jit(solution)/shard_map/ppermute | solution.py:376
  (93 shorter events, 15.8 us)
Async XLA Ops:
  0.0 152.2 %copy-start = (bf16[1,512,1664]{2,1,0:T(8,128)(2,1)S(1)}, bf16[1,512,1664]{2,1,0:T(8,128)(2,1)}, u32[]{:S(2)}) copy-start(bf16[1,512,1664]{2,1,0:T(8,128)(2,1)} %param.21) | copy-start | bytes 5111812
  1.2 40.5 %collective-permute-start = (bf16[104,217]{0,1:T(8,128)(2,1)S(1)}, bf16[104,217]{0,1:T(8,128)(2,1)S(1)}, u32[]{:S(2)}, u32[]{:S(2)}) collective-permute-start(bf16[104,217]{0,1:T(8,128)(2,1)S(1)} %slice.92), channel_id=1, source_target_pairs={{1,0},{2,1},{3,2},{4,3},{5,4},{6,5},{7,6},{8,7},{9,8},{10,9},{11,1... | collective-permute-start | bytes 135416 | tf_op jit(solution)/shard_map/ppermute | solution.py:376
  33.7 1.2 copy-start.11
  34.9 1.4 copy-start.9
  34.9 1.6 copy-start.6
  34.9 1.6 copy-start.8
  36.1 4.4 %copy-start.7 = (f32[104,32]{0,1:T(8,128)S(1)}, f32[104,32]{0,1:T(8,128)}, u32[]{:S(2)}) copy-start(f32[104,32]{0,1:T(8,128)} %param.19) | copy-start | bytes 39940
  36.2 4.3 %copy-start.10 = (f32[104]{0:T(128)S(1)}, f32[104]{0:T(128)}, u32[]{:S(2)}) copy-start(f32[104]{0:T(128)} %param.18) | copy-start | bytes 1252
  36.2 6.0 %collective-permute-start.1 = (bf16[3,104,217]{2,1,0:T(8,128)(2,1)S(1)}, bf16[3,104,217]{2,1,0:T(8,128)(2,1)S(1)}, u32[]{:S(2)}, u32[]{:S(2)}) collective-permute-start(bf16[3,104,217]{2,1,0:T(8,128)(2,1)S(1)} %slice.94), channel_id=1, source_target_pairs={{1,0},{2,1},{3,2},{4,3},{5,4},{6,5},{7,6},{8,7},{9,8},{10,9},{11,1... | collective-permute-start | bytes 406232 | tf_op jit(solution)/shard_map/ppermute | solution.py:376
  46.0 28.1 %copy-start.4 = (bf16[1664,104]{0,1:T(8,128)(2,1)S(1)}, bf16[1664,104]{0,1:T(8,128)(2,1)}, u32[]{:S(2)}) copy-start(bf16[1664,104]{0,1:T(8,128)(2,1)} %param.17) | copy-start | bytes 1038340
  150.3 1.9 copy-start.2
  172.3 2.1 copy-start.1
  228.1 3.9 %copy-start.3 = (pred[2,1280,1152]{2,1,0:T(32,128)(4,1)S(1)}, pred[2,1280,1152]{2,1,0:T(32,128)(4,1)}, u32[]{:S(2)}) copy-start(pred[2,1280,1152]{2,1,0:T(32,128)(4,1)} %iota_compare_fusion) | copy-start | bytes 8847364
  228.1 3.9 %copy-start.5 = (bf16[32,40,104]{2,1,0:T(8,128)(2,1)S(1)}, bf16[32,40,104]{2,1,0:T(8,128)(2,1)}, u32[]{:S(2)}) copy-start(bf16[32,40,104]{2,1,0:T(8,128)(2,1)} %exchange_7.1) | copy-start | bytes 798724
  236.8 4.8 %collective-permute-start.2 = (bf16[104,217]{1,0:T(8,128)(2,1)S(1)}, bf16[104,217]{1,0:T(8,128)(2,1)S(1)}, u32[]{:S(2)}, u32[]{:S(2)}) collective-permute-start(bf16[104,217]{1,0:T(8,128)(2,1)S(1)} %slice.153), channel_id=1, source_target_pairs={{31,0},{0,1},{1,2},{2,3},{3,4},{4,5},{5,6},{6,7},{7,8},{8,9},{9,10... | collective-permute-start | bytes 135416 | tf_op jit(solution)/shard_map/ppermute | solution.py:376
